TPU v7x, 512 devices: a whole 4x4x16 slice. The times are simulated.
512 devices in a mesh: head: 8 (over y, x_hi), seq: 16 (over z), dp: 4 (over x_lo, core).
Axes of the slice: x: 4 (x_hi: 2, x_lo: 2; x = x_hi * 2 + x_lo), y: 4, z: 16, core: 2. Of those that a mesh axis runs over, the one named last changes fastest.
Arguments:
- teacher_query: bfloat16 [4, 2048, 3072], P('dp', 'seq', 'head'), may hold values from -6 to 6
- teacher_key: bfloat16 [4, 2048, 3072], P('dp', 'seq', 'head'), may hold values from -6 to 6
- student_query: bfloat16 [4, 2048, 512], P('dp', 'seq'), may hold values from -6 to 6
- student_key: bfloat16 [4, 2048, 512], P('dp', 'seq'), may hold values from -6 to 6
- head_mix: float32 [24, 8], P('head'), may hold values from 0.02 to 0.25
Outputs:
- grad_query: float32 [4, 2048, 512], P('dp', 'seq', 'head')
- grad_key: float32 [4, 2048, 512], P('dp', 'seq', 'head')
- grad_mix: float32 [24, 8], P('head')
- head_loss: float32 [24], P('head')
All inputs are finite; a program needn't handle non-finite values.
Results may differ from a plain program's by a relative error of at most 0.0012.
Values may be sent and summed in bfloat16 or wider, within the bound.
A program may use at most 64 MiB of HBM per device.

v0:
```python
import math

import jax
import jax.numpy as jnp
from jax import lax
from jax.sharding import PartitionSpec as P

HEADS_T = 24
HD_T = 128
HEADS_S = 8
HD_S = 64


def from_behind(block, axis, distance):
    devices = range(lax.axis_size(axis))
    route = [((i - distance) % len(devices), i) for i in devices]
    return lax.ppermute(block, axis, route)


def lift_heads(head_mix, student):
    lifted = head_mix[:, 0, None, None] * student[0][None]
    for index in range(1, HEADS_S):
        lifted = lifted + head_mix[:, index, None, None] * student[index][None]
    return lifted


def block_maps(query_t, query_s, key_t, key_s, head_mix):
    row_count = query_t.shape[0]
    key_count = key_t.shape[0]
    teacher_heads = head_mix.shape[0]
    teacher = jnp.einsum(
        "rhd,khd->hrk",
        query_t.reshape(row_count, teacher_heads, HD_T),
        key_t.reshape(key_count, teacher_heads, HD_T),
        preferred_element_type=jnp.float32,
    ) * HD_T ** (-0.5)
    student = jnp.einsum(
        "rhd,khd->hrk",
        query_s.reshape(row_count, HEADS_S, HD_S),
        key_s.reshape(key_count, HEADS_S, HD_S),
        preferred_element_type=jnp.float32,
    ) * HD_S ** (-0.5)
    lifted = lift_heads(head_mix, student)
    return (teacher, student, lifted)


def absorb(stats, teacher, lifted):
    top_t, total_t, top_l, total_l = stats
    new_t = jnp.maximum(top_t, jnp.max(teacher, axis=-1))
    new_l = jnp.maximum(top_l, jnp.max(lifted, axis=-1))
    total_t = total_t * jnp.exp(top_t - new_t) + jnp.sum(
        jnp.exp(teacher - new_t[..., None]), axis=-1
    )
    total_l = total_l * jnp.exp(top_l - new_l) + jnp.sum(
        jnp.exp(lifted - new_l[..., None]), axis=-1
    )
    return (new_t, total_t, new_l, total_l)


def pair_terms(query_t, query_s, key_t, key_s, head_mix, lse_t, lse_l):
    teacher, student, lifted = block_maps(query_t, query_s, key_t, key_s, head_mix)
    prob_t = jnp.exp(teacher - lse_t[..., None])
    prob_l = jnp.exp(lifted - lse_l[..., None])
    kl_part = jnp.sum(prob_t * (teacher - lifted), axis=-1)
    excess = prob_l - prob_t
    mix_columns = []
    mixed_rows = []
    for index in range(HEADS_S):
        mix_columns.append(jnp.sum(excess * student[index][None], axis=(1, 2)))
        mixed_rows.append(jnp.sum(head_mix[:, index, None, None] * excess, axis=0))
    mix_part = jnp.stack(mix_columns, axis=1)
    mixed_grad = jnp.stack(mixed_rows, axis=0).astype(jnp.bfloat16)
    return (kl_part, mix_part, mixed_grad)


def query_side(mixed_grad, key_s):
    key_count = key_s.shape[0]
    result = jnp.einsum(
        "hrk,khd->rhd",
        mixed_grad,
        key_s.reshape(key_count, HEADS_S, HD_S),
        preferred_element_type=jnp.float32,
    )
    return result.reshape(result.shape[0], HEADS_S * HD_S)


def key_side(mixed_grad, query_s):
    row_count = query_s.shape[0]
    result = jnp.einsum(
        "hrk,rhd->khd",
        mixed_grad,
        query_s.reshape(row_count, HEADS_S, HD_S),
        preferred_element_type=jnp.float32,
    )
    return result.reshape(result.shape[0], HEADS_S * HD_S)


def body(teacher_query, teacher_key, student_query, student_key, head_mix):
    query_t = teacher_query[0]
    query_s = student_query[0]
    own_t = teacher_key[0]
    own_s = student_key[0]
    row_count = query_t.shape[0]
    teacher_heads = head_mix.shape[0]
    group_size = lax.axis_size("seq")
    position = lax.axis_index("seq")
    shards_per = math.gcd(group_size, max(1, 512 // row_count))
    block_rows = shards_per * row_count
    block_count = group_size // shards_per
    gathered = (
        lax.all_gather(teacher_key, "seq", axis=1, tiled=True),
        lax.all_gather(student_key, "seq", axis=1, tiled=True),
    )
    keys_t = gathered[0][0]
    keys_s = gathered[1][0]

    def first_pass(index, stats):
        start = index * block_rows
        key_t = lax.dynamic_slice_in_dim(keys_t, start, block_rows, 0)
        key_s = lax.dynamic_slice_in_dim(keys_s, start, block_rows, 0)
        teacher, student, lifted = block_maps(query_t, query_s, key_t, key_s, head_mix)
        return absorb(stats, teacher, lifted)

    floor_value = jnp.full((teacher_heads, row_count), -1e30, jnp.float32)
    zero_rows = jnp.zeros((teacher_heads, row_count), jnp.float32)
    stats = lax.fori_loop(
        0, block_count, first_pass, (floor_value, zero_rows, floor_value, zero_rows)
    )
    lse_t = stats[0] + jnp.log(stats[1])
    lse_l = stats[2] + jnp.log(stats[3])
    kl_sum, mix_sum, mixed_grad = pair_terms(query_t, query_s, own_t, own_s, head_mix, lse_t, lse_l)
    query_grad = query_side(mixed_grad, own_s)
    carried = key_side(mixed_grad, query_s)

    def second_pass(turn, carry):
        kl_acc, mix_acc, query_acc, moving = carry
        moving = from_behind(moving, "seq", 1)
        start = (position - turn) % group_size * row_count
        key_t = lax.dynamic_slice_in_dim(keys_t, start, row_count, 0)
        key_s = lax.dynamic_slice_in_dim(keys_s, start, row_count, 0)
        kl_part, mix_part, mixed = pair_terms(
            query_t, query_s, key_t, key_s, head_mix, lse_t, lse_l
        )
        return (
            kl_acc + kl_part,
            mix_acc + mix_part,
            query_acc + query_side(mixed, key_s),
            moving + key_side(mixed, query_s),
        )

    kl_sum, mix_sum, query_grad, carried = lax.fori_loop(
        1, group_size, second_pass, (kl_sum, mix_sum, query_grad, carried)
    )
    key_grad = from_behind(carried, "seq", 1)
    seq_len = row_count * group_size
    images = lax.axis_size("dp") * teacher_query.shape[0]
    weight = seq_len / HEADS_T
    factor = weight * HD_S ** (-0.5)
    grad_query, grad_key = (
        lax.psum_scatter((query_grad * factor)[None], "head", scatter_dimension=2, tiled=True),
        lax.psum_scatter((key_grad * factor)[None], "head", scatter_dimension=2, tiled=True),
    )
    kl_rows = jnp.sum(kl_sum - lse_t + lse_l, axis=-1)
    mix_total, loss_total = lax.psum((mix_sum, kl_rows), ("seq", "dp"))
    grad_mix = mix_total * (weight / (images * seq_len))
    head_loss = loss_total / (images * seq_len)
    return (grad_query, grad_key, grad_mix, head_loss)


def solution(mesh):
    return jax.shard_map(
        body,
        mesh=mesh,
        in_specs=(
            P("dp", "seq", "head"),
            P("dp", "seq", "head"),
            P("dp", "seq", None),
            P("dp", "seq", None),
            P("head", None),
        ),
        out_specs=(P("dp", "seq", "head"), P("dp", "seq", "head"), P("head", None), P("head")),
        check_vma=False,
    )
```

profile of v0, /device:TPU:1, one launch (start us, length us, event | category | flops | bytes accessed | tf_op | source)
XLA Modules:
  0.0 523.8 jit_solution(4273540421250965893)
XLA Ops:
  7.2 1.6 copy.146
  8.9 1.6 copy.150
  10.7 1.0 copy.153
  11.7 1.0 copy.145
  13.5 1.2 convolution_multiply_fusion.3
  15.8 63.9 %all-gather.3.cloned.1.call-done = bf16[1,2048,384]{1,2,0:T(8,128)(2,1)} async-done(((bf16[1,128,384]{1,2,0:T(8,128)(2,1)}), bf16[1,2048,384]{1,2,0:T(8,128)(2,1)}) %all-gather.3.cloned.1.call-update) | async-done | bytes 1572880 | tf_op jit(solution)/shard_map/all_gather | solution.py:111
  79.7 75.8 %all-gather.5.cloned.1.call-done = bf16[1,2048,512]{1,2,0:T(8,128)(2,1)} async-done(((bf16[1,128,512]{1,2,0:T(8,128)(2,1)}), bf16[1,2048,512]{1,2,0:T(8,128)(2,1)}) %all-gather.5.cloned.1.call-update) | async-done | bytes 2097168 | tf_op jit(solution)/shard_map/all_gather | solution.py:112
  155.5 22.7 %while.42 = (s32[]{:T(128)}, f32[3,128]{1,0:T(4,128)S(1)}, f32[3,128]{1,0:T(4,128)S(1)}, f32[3,128]{1,0:T(4,128)S(1)}, f32[3,128]{1,0:T(4,128)S(1)}, /*index=5*/...) while((s32[]{:T(128)}, f32[3,128]{1,0:T(4,128)S(1)}, ...), condition=%wide.region_5.0_spmd.clone, body=%wide.region_0.0_spmd.clone.sunk | while | flops 125243136 | bytes 19275332 | solution.py:126
  155.5 1.1 constant_dynamic-slice_fusion.11
  159.7 1.0 constant_dynamic-slice_fusion.10
  161.3 1.1 constant_dynamic-slice_fusion.11
  165.4 1.0 constant_dynamic-slice_fusion.10
  166.9 1.1 constant_dynamic-slice_fusion.11
  171.0 1.0 constant_dynamic-slice_fusion.10
  172.6 1.1 constant_dynamic-slice_fusion.11
  176.7 1.0 constant_dynamic-slice_fusion.10
  180.7 138.2 %while.41 = (s32[]{:T(128)}, f32[3,128]{1,0:T(4,128)S(1)}, f32[3,8]{0,1:T(8,128)S(1)}, f32[128,512]{0,1:T(8,128)S(1)}, f32[128,512]{0,1:T(8,128)S(1)}, /*index=5...) while((s32[]{:T(128)}, f32[3,128]{1,0:T(4,128)S(1)}, ...), condition=%wide.region_41.42_spmd, body=%wide.region_23.41_spmd.sunk | while | flops 66486288 | bytes 9580356 | solution.py:151
  180.7 3.5 collective-permute-start
  184.2 0.9 constant_dynamic-slice_fusion.8
  189.1 2.4 collective-permute-start
  191.5 0.9 constant_dynamic-slice_fusion.8
  196.1 1.3 collective-permute-done
  197.4 1.9 collective-permute-start
  199.4 0.9 constant_dynamic-slice_fusion.8
  204.0 1.7 collective-permute-done
  205.8 1.9 collective-permute-start
  207.8 0.9 constant_dynamic-slice_fusion.8
  212.4 2.1 collective-permute-done
  214.5 1.9 collective-permute-start
  216.5 0.9 constant_dynamic-slice_fusion.8
  221.1 3.3 collective-permute-done
  224.4 1.9 collective-permute-start
  226.3 0.9 constant_dynamic-slice_fusion.8
  230.9 4.5 collective-permute-done
  235.5 1.9 collective-permute-start
  237.5 0.9 constant_dynamic-slice_fusion.8
  242.1 4.0 collective-permute-done
  246.1 1.9 collective-permute-start
  248.1 0.9 constant_dynamic-slice_fusion.8
  252.7 3.2 collective-permute-done
  255.9 1.9 collective-permute-start
  257.8 0.9 constant_dynamic-slice_fusion.8
  262.5 2.3 collective-permute-done
  264.8 1.9 collective-permute-start
  266.8 0.9 constant_dynamic-slice_fusion.8
  271.4 1.8 collective-permute-done
  273.2 1.9 collective-permute-start
  275.1 0.9 constant_dynamic-slice_fusion.8
  279.7 1.8 collective-permute-done
  281.5 1.9 collective-permute-start
  283.5 0.9 constant_dynamic-slice_fusion.8
  288.1 1.8 collective-permute-done
  289.9 1.9 collective-permute-start
  291.9 0.9 constant_dynamic-slice_fusion.8
  296.5 1.9 collective-permute-done
  298.4 1.9 collective-permute-start
  300.4 0.9 constant_dynamic-slice_fusion.8
  305.0 3.1 collective-permute-done
  308.1 1.9 collective-permute-start
  314.7 4.2 collective-permute-done
  319.7 1.9 collective-permute-start.1
  321.7 9.4 %collective-permute-done.1 = f32[128,512]{0,1:T(8,128)S(1)} collective-permute-done((f32[128,512]{0,1:T(8,128)S(1)}, f32[128,512]{0,1:T(8,128)S(1)}, u32[]{:S(2)}, u32[]{:S(2)}) %collective-permute-start.1) | collective-permute-done | bytes 262176 | tf_op jit(solution)/shard_map/ppermute | solution.py:17
  332.0 133.8 %all-reduce = (f32[3,8]{1,0:T(4,128)S(1)}, f32[3]{0:T(128)S(1)}) all-reduce(f32[3,8]{1,0:T(4,128)S(1)} %copy.175, f32[3]{0:T(128)S(1)} %add_reduce_fusion), channel_id=1, replica_groups=mesh['head'=8,'seq'=16,'dp'=4] {'seq','dp'}, use_global_device_ids=true, to_apply=%region_44.45 | all-reduce | flops 27 | bytes 216 | tf_op jit(solution)/shard_map/psum | solution.py:164
  466.9 50.4 %reduce-scatter.5.cloned.1.call-done = f32[1,128,64]{1,2,0:T(8,128)} async-done(((f32[1,128,512]{1,2,0:T(8,128)}), f32[1,128,64]{1,2,0:T(8,128)}) %reduce-scatter.5.cloned.1.call-update) | async-done | bytes 32784 | tf_op jit(solution)/shard_map/reduce_scatter | solution.py:161
  (575 shorter events, 75.5 us)
Async XLA Ops:
  7.2 8.4 %copy-start.2 = (f32[3,8]{1,0:T(4,128)S(1)}, f32[3,8]{1,0:T(4,128)}, u32[]{:S(2)}) copy-start(f32[3,8]{1,0:T(4,128)} %param.13) | copy-start | bytes 292
  7.2 72.5 %all-gather.3.cloned.1.call-start = ((), (), s32[]{:S(2)}) async-start(), calls=%async_computation.2 | async-start | bytes 1671168 | tf_op jit(solution)/shard_map/all_gather | solution.py:111
  8.9 146.7 %all-gather.5.cloned.1.call-start = ((), (), s32[]{:S(2)}) async-start(), calls=%async_computation.3 | async-start | bytes 2228224 | tf_op jit(solution)/shard_map/all_gather | solution.py:112
  10.6 456.3 %reduce-scatter.3.cloned.1.call-start = ((), (), s32[]{:S(2)}) async-start(), calls=%async_computation.4 | async-start | bytes 294912 | tf_op jit(solution)/shard_map/reduce_scatter | solution.py:160
  155.5 22.8 %copy-start.1 = (bf16[1,128,384]{1,2,0:T(8,128)(2,1)S(1)}, bf16[1,128,384]{1,2,0:T(8,128)(2,1)}, u32[]{:S(2)}) copy-start(bf16[1,128,384]{1,2,0:T(8,128)(2,1)} %copy.146) | copy-start | bytes 294916
  178.3 2.1 copy-start
  180.7 8.3 %collective-permute-start = (f32[128,512]{0,1:T(8,128)S(1)}, f32[128,512]{0,1:T(8,128)S(1)}, u32[]{:S(2)}, u32[]{:S(2)}) collective-permute-start(f32[128,512]{0,1:T(8,128)S(1)} %get-tuple-element.1076), channel_id=1, source_target_pairs={{60,0},{0,4},{4,8},{8,12},{12,16},{16,20},{20,24},{24,28},{28,32},... | collective-permute-start | bytes 786440 | tf_op jit(solution)/shard_map/while/body/eval_jaxpr/ppermute | solution.py:17
  189.1 8.3 %collective-permute-start = (f32[128,512]{0,1:T(8,128)S(1)}, f32[128,512]{0,1:T(8,128)S(1)}, u32[]{:S(2)}, u32[]{:S(2)}) collective-permute-start(f32[128,512]{0,1:T(8,128)S(1)} %get-tuple-element.1076), channel_id=1, source_target_pairs={{60,0},{0,4},{4,8},{8,12},{12,16},{16,20},{20,24},{24,28},{28,32},... | collective-permute-start | bytes 786440 | tf_op jit(solution)/shard_map/while/body/eval_jaxpr/ppermute | solution.py:17
  197.4 8.3 %collective-permute-start = (f32[128,512]{0,1:T(8,128)S(1)}, f32[128,512]{0,1:T(8,128)S(1)}, u32[]{:S(2)}, u32[]{:S(2)}) collective-permute-start(f32[128,512]{0,1:T(8,128)S(1)} %get-tuple-element.1076), channel_id=1, source_target_pairs={{60,0},{0,4},{4,8},{8,12},{12,16},{16,20},{20,24},{24,28},{28,32},... | collective-permute-start | bytes 786440 | tf_op jit(solution)/shard_map/while/body/eval_jaxpr/ppermute | solution.py:17
  205.8 8.7 %collective-permute-start = (f32[128,512]{0,1:T(8,128)S(1)}, f32[128,512]{0,1:T(8,128)S(1)}, u32[]{:S(2)}, u32[]{:S(2)}) collective-permute-start(f32[128,512]{0,1:T(8,128)S(1)} %get-tuple-element.1076), channel_id=1, source_target_pairs={{60,0},{0,4},{4,8},{8,12},{12,16},{16,20},{20,24},{24,28},{28,32},... | collective-permute-start | bytes 786440 | tf_op jit(solution)/shard_map/while/body/eval_jaxpr/ppermute | solution.py:17
  214.5 9.8 %collective-permute-start = (f32[128,512]{0,1:T(8,128)S(1)}, f32[128,512]{0,1:T(8,128)S(1)}, u32[]{:S(2)}, u32[]{:S(2)}) collective-permute-start(f32[128,512]{0,1:T(8,128)S(1)} %get-tuple-element.1076), channel_id=1, source_target_pairs={{60,0},{0,4},{4,8},{8,12},{12,16},{16,20},{20,24},{24,28},{28,32},... | collective-permute-start | bytes 786440 | tf_op jit(solution)/shard_map/while/body/eval_jaxpr/ppermute | solution.py:17
  224.4 11.1 %collective-permute-start = (f32[128,512]{0,1:T(8,128)S(1)}, f32[128,512]{0,1:T(8,128)S(1)}, u32[]{:S(2)}, u32[]{:S(2)}) collective-permute-start(f32[128,512]{0,1:T(8,128)S(1)} %get-tuple-element.1076), channel_id=1, source_target_pairs={{60,0},{0,4},{4,8},{8,12},{12,16},{16,20},{20,24},{24,28},{28,32},... | collective-permute-start | bytes 786440 | tf_op jit(solution)/shard_map/while/body/eval_jaxpr/ppermute | solution.py:17
  235.5 10.6 %collective-permute-start = (f32[128,512]{0,1:T(8,128)S(1)}, f32[128,512]{0,1:T(8,128)S(1)}, u32[]{:S(2)}, u32[]{:S(2)}) collective-permute-start(f32[128,512]{0,1:T(8,128)S(1)} %get-tuple-element.1076), channel_id=1, source_target_pairs={{60,0},{0,4},{4,8},{8,12},{12,16},{16,20},{20,24},{24,28},{28,32},... | collective-permute-start | bytes 786440 | tf_op jit(solution)/shard_map/while/body/eval_jaxpr/ppermute | solution.py:17
  246.1 9.7 %collective-permute-start = (f32[128,512]{0,1:T(8,128)S(1)}, f32[128,512]{0,1:T(8,128)S(1)}, u32[]{:S(2)}, u32[]{:S(2)}) collective-permute-start(f32[128,512]{0,1:T(8,128)S(1)} %get-tuple-element.1076), channel_id=1, source_target_pairs={{60,0},{0,4},{4,8},{8,12},{12,16},{16,20},{20,24},{24,28},{28,32},... | collective-permute-start | bytes 786440 | tf_op jit(solution)/shard_map/while/body/eval_jaxpr/ppermute | solution.py:17
  255.9 8.9 %collective-permute-start = (f32[128,512]{0,1:T(8,128)S(1)}, f32[128,512]{0,1:T(8,128)S(1)}, u32[]{:S(2)}, u32[]{:S(2)}) collective-permute-start(f32[128,512]{0,1:T(8,128)S(1)} %get-tuple-element.1076), channel_id=1, source_target_pairs={{60,0},{0,4},{4,8},{8,12},{12,16},{16,20},{20,24},{24,28},{28,32},... | collective-permute-start | bytes 786440 | tf_op jit(solution)/shard_map/while/body/eval_jaxpr/ppermute | solution.py:17
  264.8 8.3 %collective-permute-start = (f32[128,512]{0,1:T(8,128)S(1)}, f32[128,512]{0,1:T(8,128)S(1)}, u32[]{:S(2)}, u32[]{:S(2)}) collective-permute-start(f32[128,512]{0,1:T(8,128)S(1)} %get-tuple-element.1076), channel_id=1, source_target_pairs={{60,0},{0,4},{4,8},{8,12},{12,16},{16,20},{20,24},{24,28},{28,32},... | collective-permute-start | bytes 786440 | tf_op jit(solution)/shard_map/while/body/eval_jaxpr/ppermute | solution.py:17
  273.2 8.3 %collective-permute-start = (f32[128,512]{0,1:T(8,128)S(1)}, f32[128,512]{0,1:T(8,128)S(1)}, u32[]{:S(2)}, u32[]{:S(2)}) collective-permute-start(f32[128,512]{0,1:T(8,128)S(1)} %get-tuple-element.1076), channel_id=1, source_target_pairs={{60,0},{0,4},{4,8},{8,12},{12,16},{16,20},{20,24},{24,28},{28,32},... | collective-permute-start | bytes 786440 | tf_op jit(solution)/shard_map/while/body/eval_jaxpr/ppermute | solution.py:17
  281.5 8.3 %collective-permute-start = (f32[128,512]{0,1:T(8,128)S(1)}, f32[128,512]{0,1:T(8,128)S(1)}, u32[]{:S(2)}, u32[]{:S(2)}) collective-permute-start(f32[128,512]{0,1:T(8,128)S(1)} %get-tuple-element.1076), channel_id=1, source_target_pairs={{60,0},{0,4},{4,8},{8,12},{12,16},{16,20},{20,24},{24,28},{28,32},... | collective-permute-start | bytes 786440 | tf_op jit(solution)/shard_map/while/body/eval_jaxpr/ppermute | solution.py:17
  289.9 8.5 %collective-permute-start = (f32[128,512]{0,1:T(8,128)S(1)}, f32[128,512]{0,1:T(8,128)S(1)}, u32[]{:S(2)}, u32[]{:S(2)}) collective-permute-start(f32[128,512]{0,1:T(8,128)S(1)} %get-tuple-element.1076), channel_id=1, source_target_pairs={{60,0},{0,4},{4,8},{8,12},{12,16},{16,20},{20,24},{24,28},{28,32},... | collective-permute-start | bytes 786440 | tf_op jit(solution)/shard_map/while/body/eval_jaxpr/ppermute | solution.py:17
  298.4 9.6 %collective-permute-start = (f32[128,512]{0,1:T(8,128)S(1)}, f32[128,512]{0,1:T(8,128)S(1)}, u32[]{:S(2)}, u32[]{:S(2)}) collective-permute-start(f32[128,512]{0,1:T(8,128)S(1)} %get-tuple-element.1076), channel_id=1, source_target_pairs={{60,0},{0,4},{4,8},{8,12},{12,16},{16,20},{20,24},{24,28},{28,32},... | collective-permute-start | bytes 786440 | tf_op jit(solution)/shard_map/while/body/eval_jaxpr/ppermute | solution.py:17
  308.1 10.8 %collective-permute-start = (f32[128,512]{0,1:T(8,128)S(1)}, f32[128,512]{0,1:T(8,128)S(1)}, u32[]{:S(2)}, u32[]{:S(2)}) collective-permute-start(f32[128,512]{0,1:T(8,128)S(1)} %get-tuple-element.1076), channel_id=1, source_target_pairs={{60,0},{0,4},{4,8},{8,12},{12,16},{16,20},{20,24},{24,28},{28,32},... | collective-permute-start | bytes 786440 | tf_op jit(solution)/shard_map/while/body/eval_jaxpr/ppermute | solution.py:17
  319.7 197.6 %reduce-scatter.5.cloned.1.call-start = ((), (), s32[]{:S(2)}) async-start(), calls=%async_computation.5 | async-start | bytes 294912 | tf_op jit(solution)/shard_map/reduce_scatter | solution.py:161
  319.7 11.4 %collective-permute-start.1 = (f32[128,512]{0,1:T(8,128)S(1)}, f32[128,512]{0,1:T(8,128)S(1)}, u32[]{:S(2)}, u32[]{:S(2)}) collective-permute-start(f32[128,512]{0,1:T(8,128)S(1)} %get-tuple-element.493), channel_id=1, source_target_pairs={{60,0},{0,4},{4,8},{8,12},{12,16},{16,20},{20,24},{24,28},{28,32},... | collective-permute-start | bytes 786440 | tf_op jit(solution)/shard_map/ppermute | solution.py:17
Sparse Core Ops, SparseCore 0:
  10.0 69.6 all-gather.2
  81.7 73.7 all-gather.4
  319.8 107.5 reduce-scatter.2
  432.2 85.0 reduce-scatter.4
where the time goes:
time: 526 us; the launch traced here: 524 us
  waiting for transfers between devices  237 us (45%)
  blocking collectives  134 us (25%)
  local copies, waits for them, and re-layouts  65.5 us (12%)
  starting transfers between devices  32.9 us (6%)
  matrix products  20.9 us (4%)
  other arithmetic  16.5 us (3%)
  between operations  14.1 us (3%)
    psum x1, blocking collectives, body(): mix_total, loss_total = lax.psum((mix_sum, kl_rows), ('seq', 'dp'))  134 us
    all_gather x1, waiting for transfers between devices, body(): lax.all_gather(student_key, 'seq', axis=1, tiled=True)  75.8 us
    all_gather x1, waiting for transfers between devices, body(): lax.all_gather(teacher_key, 'seq', axis=1, tiled=True)  63.9 us
    reduce_scatter x1, waiting for transfers between devices, body(): lax.psum_scatter((key_grad * factor)[None], 'head', scatter_dimension=2,...  50.4 us
    ppermute x16, waiting for transfers between devices, from_behind(): return lax.ppermute(block, axis, route)  46.6 us
    ppermute x16, starting transfers between devices, from_behind(): return lax.ppermute(block, axis, route)  32.7 us
    reduce_sum x128, local copies, waits for them, and re-layouts, pair_terms(): mixed_rows.append(jnp.sum(head_mix[:, index, None, None] * excess, axis=0))  15.2 us
    dynamic_slice x15, local copies, waits for them, and re-layouts, second_pass(): key_s = lax.dynamic_slice_in_dim(keys_s, start, row_count, 0)  13.8 us
  transfers between devices with their start and end apart: 20, of which 19 were waited for; matrix products, arithmetic and copies ran while one was open for 14% of the time, Pallas kernels for 0%

commit v1 on v0

v1 whole, which is shorter than its diff:
```python
import functools

import jax
import jax.numpy as jnp
from jax import lax
from jax.experimental import pallas as pl
from jax.experimental.pallas import tpu as pltpu
from jax.sharding import PartitionSpec as P

HEADS_T = 24
HD_T = 128
HEADS_S = 8
HD_S = 64
MESH = pl.DeviceIdType.MESH
NT = (((1,), (1,)), ((), ()))
F32 = jnp.float32
VM = pltpu.VMEM
WHOLE = pl.BlockSpec(memory_space=pltpu.VMEM)
ANY = pl.BlockSpec(memory_space=pl.ANY)
SMEM = pl.BlockSpec(memory_space=pltpu.SMEM)
COLS = 2


def ring(axis, shift):
    n = lax.axis_size(axis)
    return lax.rem(lax.axis_index(axis) + (shift + n), n)


def remote(src, dst, send, recv, where):
    return pltpu.make_async_remote_copy(
        src_ref=src, dst_ref=dst, send_sem=send, recv_sem=recv,
        device_id=where, device_id_type=MESH)


def greet(places):
    barrier = pltpu.get_barrier_semaphore()
    for place in places:
        pl.semaphore_signal(barrier, inc=1, device_id=place, device_id_type=MESH)
    pl.semaphore_wait(barrier, len(places))


class Gather:
    def __init__(self, which, t_own, s_own, t_all, s_all, sems):
        self.which = which
        self.t_own, self.s_own, self.t_all, self.s_all = t_own, s_own, t_all, s_all
        self.ts, self.tr, self.zs, self.zr, self.ys, self.yr, self.local = sems
        self.n = lax.axis_size("seq")
        self.half = self.n // 2
        self.z = lax.axis_index("seq")
        g = lax.axis_index("head")
        self.rows = t_own.shape[0]
        self.ny = lax.axis_size("head") // COLS
        self.y = g // COLS
        self.x = lax.rem(g, COLS)
        self.sent = []

    def y_at(self, shift):
        return lax.rem(self.y + (shift + self.ny), self.ny)

    def y_place(self, shift):
        return {"head": self.y_at(shift) * COLS + self.x}

    def shard(self, way, s):
        return ring("seq", -s if way == 0 else s)

    def t_has(self, way, s, c):
        return s < self.half or (s == self.half and way == c)

    def s_has(self, way, s):
        return s < self.half or (s == self.half and way == self.which)

    def t_copy(self, way, s, c):
        step = self.rows // 2
        part = pl.ds(c * step, step)
        i = self.shard(way, s - 1)
        src = self.t_own.at[part] if s == 1 else self.t_all.at[i, part]
        return remote(src, self.t_all.at[i, part], self.ts.at[self.which, way, s, c],
                      self.tr.at[self.which, way, s, c],
                      {"seq": ring("seq", 1 if way == 0 else -1)})

    def s_piece(self):
        return self.s_own.at[:, pl.ds(pl.multiple_of(self.y * 128, 128), 128)]

    def s_copy(self, way, s):
        i = self.shard(way, s - 1)
        src = self.s_piece() if s == 1 else self.s_all.at[i, self.y]
        return remote(src, self.s_all.at[i, self.y], self.zs.at[self.which, way, s],
                      self.zr.at[self.which, way, s],
                      {"seq": ring("seq", 1 if way == 0 else -1)})

    def y_copy(self, way, s, hop):
        i = self.shard(way, s)
        to = 1
        q = self.y
        if hop == 1:
            to = -1
        if hop == 2:
            to = 1 if (s + way + self.which) % 2 == 0 else -1
            q = self.y_at(-to)
        src = self.s_piece() if s == 0 and hop < 2 else self.s_all.at[i, q]
        return remote(src, self.s_all.at[i, q], self.ys.at[self.which, way, s, hop],
                      self.yr.at[self.which, way, s, hop], self.y_place(to))

    def go(self, copy):
        copy.start()
        self.sent.append(copy)

    def ways(self, s):
        return [0] if s == 0 else [w for w in (0, 1) if self.s_has(w, s)]

    def begin(self):
        self.locals = [
            pltpu.make_async_copy(self.t_own, self.t_all.at[self.z], self.local.at[self.which, 0]),
        ]
        for q in range(self.ny):
            self.locals.append(pltpu.make_async_copy(
                self.s_own.at[:, q * 128:(q + 1) * 128], self.s_all.at[self.z, q], self.local.at[self.which, 1 + q]))
        for way in (0, 1):
            if self.s_has(way, 1):
                self.go(self.s_copy(way, 1))
        for way in (0, 1):
            for c in ((0, 1) if way == 0 else (1, 0)):
                if self.t_has(way, 1, c):
                    self.go(self.t_copy(way, 1, c))
        for c in self.locals:
            c.start()

    def s_step(self, s):
        for way in self.ways(s):
            self.s_copy(way, s).wait_recv()
            if self.s_has(way, s + 1):
                self.go(self.s_copy(way, s + 1))
            for hop in (0, 1):
                self.go(self.y_copy(way, s, hop))

    def y_step(self, s):
        for way in self.ways(s):
            self.y_copy(way, s, 0).wait_recv()
            self.y_copy(way, s, 1).wait_recv()
            self.go(self.y_copy(way, s, 2))

    def y_last(self, s):
        for way in self.ways(s):
            self.y_copy(way, s, 2).wait_recv()

    def t_step(self, s):
        for c in (0, 1):
            for way in ((0, 1) if c == 0 else (1, 0)):
                if self.t_has(way, s, c):
                    self.t_copy(way, s, c).wait_recv()
                    if self.t_has(way, s + 1, c):
                        self.go(self.t_copy(way, s + 1, c))

    def step(self, s):
        if s == 0:
            self.begin()
            return
        if s <= self.half:
            self.s_step(s)
        if 1 <= s - 1 <= self.half:
            self.y_step(s - 1)
        if 1 <= s - 2 <= self.half:
            self.y_last(s - 2)
        if s <= self.half:
            self.t_step(s)

    def finish(self):
        for c in self.locals:
            c.wait()
        for c in self.sent:
            c.wait_send()


def gather_kernel(tk, sk, tq, sq, tk_all, sk_all, tq_all, sq_all, *sems):
    n = lax.axis_size("seq")
    half = n // 2
    key = Gather(0, tk, sk, tk_all, sk_all, sems)
    query = Gather(1, tq, sq, tq_all, sq_all, sems)
    greet([{"seq": ring("seq", 1)}, {"seq": ring("seq", -1)}, key.y_place(1), key.y_place(-1)])
    for s in range(half):
        key.step(s)
    query.step(0)
    for s in range(half + 2 + 1):
        if s + half <= half + 2:
            key.step(s + half)
        query.step(s + 1)
    key.finish()
    query.finish()


def gather_sems(n):
    half = n // 2
    dma = pltpu.SemaphoreType.DMA
    return [dma((2, 2, half + 1, 2)), dma((2, 2, half + 1, 2)), dma((2, 2, half + 1)),
            dma((2, 2, half + 1)), dma((2, 2, half + 1, 3)), dma((2, 2, half + 1, 3)), dma((2, 5))]


def student_piece(ref, j, h):
    lanes = (h % 2) * HD_S
    return ref[j, h // 2, :, lanes:lanes + HD_S]


def row_logits(j, tq, sq, tk_all, sk_all, t_map, s_map):
    rows = tq.shape[0]
    lanes = pl.ds(pl.multiple_of(j * rows, rows), rows)
    for t in range(t_map.shape[0]):
        cols = slice(t * HD_T, (t + 1) * HD_T)
        t_map[t, :, lanes] = lax.dot_general(
            tq[:, cols], tk_all[j, :, cols], NT, preferred_element_type=F32) * HD_T ** -0.5
    for h in range(HEADS_S):
        s_map[h, :, lanes] = lax.dot_general(
            sq[:, h * HD_S:(h + 1) * HD_S], student_piece(sk_all, j, h), NT, preferred_element_type=F32)


RB = 16
WD = 128


def lift(mix, s):
    out = []
    for t in range(3):
        acc = mix[t][0] * s[0]
        for h in range(1, HEADS_S):
            acc = acc + mix[t][h] * s[h]
        out.append(acc)
    return out


def fold(mix, ex):
    return [mix[0][h] * ex[0] + mix[1][h] * ex[1] + mix[2][h] * ex[2] for h in range(HEADS_S)]


def mixes(mix, scale):
    return [[mix[t, h] * scale for h in range(HEADS_S)] for t in range(3)]


def row_piece(rb, mix_ref, t_map, s_map, l_map, et_map, el_map, back, stat, gm):
    heads = range(3)
    steps = t_map.shape[2] // WD
    rows = pl.ds(pl.multiple_of(rb * RB, RB), RB)
    m8 = mixes(mix_ref, HD_S ** -0.5)
    m1 = mixes(mix_ref, 1.0)

    def at(j):
        return pl.ds(pl.multiple_of(j * WD, WD), WD)

    def first(j, c):
        s = [s_map[h, rows, at(j)] for h in range(HEADS_S)]
        low = lift(m8, s)
        out = []
        for t in heads:
            l_map[t, :, at(j)] = low[t]
            out.append(jnp.maximum(c[t], t_map[t, rows, at(j)]))
        for t in heads:
            out.append(jnp.maximum(c[3 + t], low[t]))
        return tuple(out)

    floor = jnp.full((RB, WD), -1e30, F32)
    tops = lax.fori_loop(0, steps, first, (floor,) * 6)
    tops = [jnp.max(v, axis=-1, keepdims=True) for v in tops]
    wide = [jnp.broadcast_to(v, (RB, WD)) for v in tops]

    def second(j, c):
        out = list(c)
        for t in heads:
            a = t_map[t, rows, at(j)]
            b = l_map[t, :, at(j)]
            ea = jnp.exp(a - wide[t])
            eb = jnp.exp(b - wide[3 + t])
            et_map[t, :, at(j)] = ea
            el_map[t, :, at(j)] = eb
            out[t] = c[t] + ea
            out[3 + t] = c[3 + t] + eb
            out[6 + t] = c[6 + t] + ea * (a - b)
        return tuple(out)

    zero = jnp.zeros((RB, WD), F32)
    sums = lax.fori_loop(0, steps, second, (zero,) * 9)
    sums = [jnp.sum(v, axis=-1, keepdims=True) for v in sums]
    lane = lax.broadcasted_iota(jnp.int32, (RB, 128), 1)
    tile = jnp.zeros((RB, 128), F32)
    inv = [jnp.broadcast_to(1.0 / sums[k], (RB, WD)) for k in range(6)]
    for t in heads:
        lt = tops[t] + jnp.log(sums[t])
        ll = tops[3 + t] + jnp.log(sums[3 + t])
        kl = sums[6 + t] / sums[t] - lt + ll
        tile = jnp.where(lane == t, lt, tile)
        tile = jnp.where(lane == 3 + t, ll, tile)
        tile = jnp.where(lane == 8 + t, kl, tile)
    stat[rows, :] = tile

    def third(j, c):
        ex = [el_map[t, :, at(j)] * inv[3 + t] - et_map[t, :, at(j)] * inv[t] for t in heads]
        out = []
        for h in range(HEADS_S):
            s = s_map[h, rows, at(j)]
            for t in heads:
                p = ex[t] * s
                out.append(c[h * 3 + t] + (p[:8] + p[8:]))
            back[h, rows, at(j)] = (m1[0][h] * ex[0] + m1[1][h] * ex[1] + m1[2][h] * ex[2]).astype(jnp.bfloat16)
        return tuple(out)

    accs = lax.fori_loop(0, steps, third, (jnp.zeros((8, WD), F32),) * 24)
    for h in range(HEADS_S):
        for t in heads:
            gm[t * HEADS_S + h] += accs[h * 3 + t]


def row_stats(stat, gm, turned):
    a = stat[...].T
    turned[...] = jnp.zeros_like(turned)
    turned[0:24, :] = jnp.sum(gm[...], axis=1) * HD_S ** -0.5
    turned[24:32, :] = a[8:16, :]
    v = jnp.sum(turned[...].T, axis=0, keepdims=True)
    sub = lax.broadcasted_iota(jnp.int32, (8, 128), 0)
    return jnp.where(sub == 6, v, a[0:8, :])


def packed(v):
    return jnp.concatenate([v[:64], v[64:]], axis=1)


def row_grads(back, sk_all, out, scale):
    n, _, rows, _ = sk_all.shape
    for h in range(HEADS_S):
        lanes = (h % 2) * HD_S
        s = sk_all[:, h // 2, :, lanes:lanes + HD_S].reshape(n * rows, HD_S)
        r = jnp.dot(back[h], s, preferred_element_type=F32) * scale
        out[h] = packed(r)


def row_kernel(scale, mix, tq, sq, tk_all, sk_all, gq, small, t_map, s_map, l_map, et_map, el_map, back, stat, gm, turned):
    n = tk_all.shape[0]

    def logits(j, _):
        row_logits(j, tq, sq, tk_all, sk_all, t_map, s_map)
        return 0

    lax.fori_loop(0, n, logits, 0)
    gm[...] = jnp.zeros_like(gm)

    def piece(rb, _):
        row_piece(rb, mix, t_map, s_map, l_map, et_map, el_map, back, stat, gm)
        return 0

    lax.fori_loop(0, tq.shape[0] // RB, piece, 0)
    small[...] = row_stats(stat, gm, turned)
    row_grads(back, sk_all, gq, scale)


def row_scratch(n, rows):
    keys = n * rows
    return [VM((3, rows, keys), F32), VM((HEADS_S, rows, keys), F32), VM((3, RB, keys), F32),
            VM((3, RB, keys), F32), VM((3, RB, keys), F32), VM((HEADS_S, rows, keys), jnp.bfloat16),
            VM((rows, 128), F32), VM((24, 8, 128), F32), VM((128, 128), F32)]


def key_shard(j, mix_ref, tk, sk, tq_all, sq_all, lse, t_map, s_map, back):
    for t in range(3):
        cols = slice(t * HD_T, (t + 1) * HD_T)
        t_map[t] = lax.dot_general(
            tk[:, cols], tq_all[j, :, cols], NT, preferred_element_type=F32) * HD_T ** -0.5
    for h in range(HEADS_S):
        s_map[h] = lax.dot_general(
            sk[:, h * HD_S:(h + 1) * HD_S], student_piece(sq_all, j, h), NT, preferred_element_type=F32)
    m8 = mixes(mix_ref, HD_S ** -0.5)
    m1 = mixes(mix_ref, 1.0)
    wide = [jnp.broadcast_to(lse[j, k:k + 1, :], (RB, 128)) for k in range(6)]
    rows = tk.shape[0]
    lanes = pl.ds(pl.multiple_of(j * rows, rows), rows)

    def block(rb, _):
        r = pl.ds(pl.multiple_of(rb * RB, RB), RB)
        low = lift(m8, [s_map[h, r, :] for h in range(HEADS_S)])
        ex = [jnp.exp(low[t] - wide[3 + t]) - jnp.exp(t_map[t, r, :] - wide[t]) for t in range(3)]
        for h, v in enumerate(fold(m1, ex)):
            back[h, r, lanes] = v.astype(jnp.bfloat16)
        return 0

    lax.fori_loop(0, rows // RB, block, 0)


def key_kernel(scale, mix, tk, sk, tq_all, sq_all, lse, gk, t_map, s_map, back):
    def shard(j, _):
        key_shard(j, mix, tk, sk, tq_all, sq_all, lse, t_map, s_map, back)
        return 0

    lax.fori_loop(0, tq_all.shape[0], shard, 0)
    row_grads(back, sq_all, gk, scale)


def stats_kernel(small, out, send, recv, local):
    n = lax.axis_size("seq")
    z = lax.axis_index("seq")
    greet([{"seq": ring("seq", o)} for o in range(1, n)])
    own = pltpu.make_async_copy(small, out.at[z], local.at[0])
    own.start()
    copies = [remote(small, out.at[z], send.at[o], recv.at[o], {"seq": ring("seq", o)}) for o in range(1, n)]
    for c in copies:
        c.start()
    own.wait()
    for o in range(1, n):
        remote(small, out.at[ring("seq", -o)], send.at[o], recv.at[o], {"seq": ring("seq", o)}).wait_recv()
    for c in copies:
        c.wait_send()


def sums_kernel(gq, gk, stats, out_q, out_k, out_m, got, mine, tiles, send, recv, dsend, drecv):
    heads = lax.axis_size("head")
    dps = lax.axis_size("dp")
    g = lax.axis_index("head")
    total = stats[0]
    for j in range(1, stats.shape[0]):
        total = total + stats[j]
    mine[...] = total
    greet([{"head": ring("head", o)} for o in range(1, heads)] + [{"dp": ring("dp", o)} for o in range(1, dps)])
    copies = []
    for o in range(1, heads):
        to = ring("head", o)
        for k, ref in enumerate((gk, gq)):
            copies.append(remote(ref.at[to], got.at[k, o], send.at[k, o], recv.at[k, o], {"head": to}))
    for o in range(1, dps):
        copies.append(remote(mine, tiles.at[o], dsend.at[o], drecv.at[o], {"dp": ring("dp", o)}))
    for c in copies:
        c.start()
    for o in range(1, dps):
        remote(mine, tiles.at[o], dsend.at[o], drecv.at[o], {"dp": ring("dp", o)}).wait_recv()
        total = total + tiles[o]
    out_m[...] = total
    for k, (ref, out) in enumerate(((gk, out_k), (gq, out_q))):
        acc = ref[g]
        for o in range(1, heads):
            remote(ref.at[0], got.at[k, o], send.at[k, o], recv.at[k, o], {"head": ring("head", o)}).wait_recv()
            acc = acc + got[k, o]
        out[0:64, :] = acc[:, 0:64]
        out[64:128, :] = acc[:, 64:128]
    for c in copies:
        c.wait_send()


def body(teacher_query, teacher_key, student_query, student_key, head_mix):
    n = lax.axis_size("seq")
    tq, sq, tk, sk = teacher_query[0], student_query[0], teacher_key[0], student_key[0]
    rows = tq.shape[0]
    bf = jnp.bfloat16
    dma = pltpu.SemaphoreType.DMA
    t_shape = jax.ShapeDtypeStruct((n, *tq.shape), bf)
    s_shape = jax.ShapeDtypeStruct((n, sq.shape[1] // 128, rows, 128), bf)
    seq_len = rows * n
    weight = seq_len / HEADS_T
    factor = weight * HD_S ** -0.5
    images = lax.axis_size("dp")

    tk_all, sk_all, tq_all, sq_all = pl.pallas_call(
        gather_kernel, out_shape=(t_shape, s_shape, t_shape, s_shape),
        in_specs=[ANY] * 4, out_specs=[ANY] * 4, scratch_shapes=gather_sems(n), name="gather",
        compiler_params=pltpu.CompilerParams(collective_id=0, has_side_effects=True),
    )(tk, sk, tq, sq)

    grads = jax.ShapeDtypeStruct((HEADS_S, rows // 2, 128), F32)
    gq, small = pl.pallas_call(
        functools.partial(row_kernel, factor), out_shape=(grads, jax.ShapeDtypeStruct((8, 128), F32)),
        in_specs=[SMEM] + [WHOLE] * 4, out_specs=[WHOLE] * 2, scratch_shapes=row_scratch(n, rows), name="rows",
    )(head_mix, tq, sq, tk_all, sk_all)

    stats = pl.pallas_call(
        stats_kernel, out_shape=jax.ShapeDtypeStruct((n, 8, 128), F32),
        in_specs=[WHOLE], out_specs=WHOLE, scratch_shapes=[dma((n,)), dma((n,)), dma((1,))], name="stats",
        compiler_params=pltpu.CompilerParams(collective_id=1, has_side_effects=True),
    )(small)

    gk = pl.pallas_call(
        functools.partial(key_kernel, factor), out_shape=grads,
        in_specs=[SMEM] + [WHOLE] * 5, out_specs=WHOLE, name="keys",
        scratch_shapes=[VM((3, rows, rows), F32), VM((HEADS_S, rows, rows), F32), VM((HEADS_S, rows, n * rows), bf)],
    )(head_mix, tk, sk, tq_all, sq_all, stats)

    heads = lax.axis_size("head")
    out = jax.ShapeDtypeStruct((rows, HD_S), F32)
    out_q, out_k, out_m = pl.pallas_call(
        sums_kernel, out_shape=(out, out, jax.ShapeDtypeStruct((8, 128), F32)),
        in_specs=[WHOLE] * 3, out_specs=[WHOLE] * 3, name="sums",
        scratch_shapes=[VM((2, heads, rows // 2, 128), F32), VM((8, 128), F32), VM((images, 8, 128), F32),
                        dma((2, heads)), dma((2, heads)), dma((images,)), dma((images,))],
        compiler_params=pltpu.CompilerParams(collective_id=2, has_side_effects=True),
    )(gq, gk, stats)
    line = out_m[6]
    grad_mix = line[0:24].reshape(3, 8) * (weight / (images * seq_len))
    head_loss = line[24:27] / (images * seq_len)
    return out_q[None], out_k[None], grad_mix, head_loss


def solution(mesh):
    return jax.shard_map(
        body,
        mesh=mesh,
        in_specs=(
            P("dp", "seq", "head"),
            P("dp", "seq", "head"),
            P("dp", "seq", None),
            P("dp", "seq", None),
            P("head", None),
        ),
        out_specs=(P("dp", "seq", "head"), P("dp", "seq", "head"), P("head", None), P("head")),
        check_vma=False,
    )
```

time: 526 us -> 160 us (0.30)
  waiting for transfers between devices: 237 us -> 0 us
  Pallas kernels: 0 us -> 153 us
  blocking collectives: 134 us -> 0 us
  local copies, waits for them, and re-layouts: 65.5 us -> 3.74 us
  starting transfers between devices: 32.9 us -> 0 us
  matrix products: 20.9 us -> 0 us
  other arithmetic: 16.5 us -> 1.96 us
  between operations: 14.1 us -> 0.66 us
    pallas_call x0 -> x5, Pallas kernels: none -> 153 us  [the longest x1 74.5 us: body(): pl.pallas_call(gather_kernel, out_shape=(t_shape, s_shape, t_shape, s_sha...]
    all_gather x2 -> x0, waiting for transfers between devices: 140 us -> none  [the longest x1 75.8 us: body(): lax.all_gather(student_key, 'seq', axis=1, tiled=True)]
    psum x1 -> x0, blocking collectives: 134 us -> none  [body(): mix_total, loss_total = lax.psum((mix_sum, kl_rows), ('seq', 'dp'))]
    reduce_scatter x2 -> x0, waiting for transfers between devices: 50.4 us -> none  [the longest x1 50.4 us: body(): lax.psum_scatter((key_grad * factor)[None], 'head', scatter_dimension=2,...]
    ppermute x16 -> x0, waiting for transfers between devices: 46.6 us -> none  [from_behind(): return lax.ppermute(block, axis, route)]
    dynamic_slice x38 -> x0, local copies, waits for them, and re-layouts: 35.9 us -> none  [the longest x15 13.8 us: second_pass(): key_s = lax.dynamic_slice_in_dim(keys_s, start, row_count, 0)]
    ppermute x16 -> x0, starting transfers between devices: 32.7 us -> none  [from_behind(): return lax.ppermute(block, axis, route)]
    dot_general x72 -> x0, matrix products: 20.9 us -> none  [the longest x20 7.41 us: block_maps(): jnp.einsum('rhd,khd->hrk', query_s.reshape(row_count, HEADS_S, HD_S), key...]
  transfers between devices with their start and end apart: 20 -> 0, of which waited for: 19 -> 0; matrix products, arithmetic and copies ran while one was open for 14% -> 0% of each run, Pallas kernels for 0% -> 0%
where the time goes in v1:
time: 160 us; the launch traced here: 159 us
  Pallas kernels  153 us (96%)
  local copies, waits for them, and re-layouts  3.74 us (2%)
  other arithmetic  1.96 us (1%)
    pallas_call x1, Pallas kernels, body(): pl.pallas_call(gather_kernel, out_shape=(t_shape, s_shape, t_shape, s_sha...  74.5 us
    pallas_call x1, Pallas kernels, body(): pl.pallas_call(sums_kernel, out_shape=(out, out, jax.ShapeDtypeStruct((8,...  24.1 us
    pallas_call x1, Pallas kernels, body(): pl.pallas_call(functools.partial(row_kernel, factor), out_shape=(grads, j...  24.1 us
    pallas_call x1, Pallas kernels, body(): pl.pallas_call(functools.partial(key_kernel, factor), out_shape=grads, in...  16.4 us
    pallas_call x1, Pallas kernels, body(): pl.pallas_call(stats_kernel, out_shape=jax.ShapeDtypeStruct((n, 8, 128),...  13.8 us

profile of v1, /device:TPU:1, one launch (start us, length us, event | category | flops | bytes accessed | tf_op | source)
XLA Modules:
  0.0 159.3 jit_solution(11874355315717729392)
XLA Ops:
  0.6 74.5 %gather.1 = (bf16[16,128,384]{2,1,0:T(8,128)(2,1)}, bf16[16,4,128,128]{3,2,1,0:T(8,128)(2,1)}, bf16[16,128,384]{2,1,0:T(8,128)(2,1)}, bf16[16,4,128,128]{3,2,1,0:T(8,128)(2,1)}) custom-call(bf16[128,384]{1,0:T(8,128)(2,1)} %bitcast.14, bf16[128,512]{1,0:T(8,128)(2,1)} %bitcast.10, bf16[128,384]{1,0:T(8,128)(2,1)} %bitcast.12, bf16[128,512]{1,0:T(8,128)(2,1)} %bitcast.8), custom_call_target="tpu_custom_call" | custom-call | tf_op jit(solution)/shard_map/gather/pallas_call | solution.py:454
  75.2 24.1 %rows.1 = (f32[8,64,128]{2,1,0:T(8,128)}, f32[8,128]{1,0:T(8,128)}) custom-call(f32[3,8]{1,0:T(4,128)} %mix.3, bf16[128,384]{1,0:T(8,128)(2,1)} %bitcast.13, bf16[128,512]{1,0:T(8,128)(2,1)} %bitcast.9, bf16[16,128,384]{2,1,0:T(8,128)(2,1)} %get-tuple-element.13.tk_all, bf16[16,4,128,128]{3,2,1,0:T(8,128)(2,1)} %get-tuple-element.14.sk_all), custom_call_target="tpu_custom_call" | custom-call | tf_op jit(solution)/shard_map/rows/pallas_call | solution.py:461
  99.3 13.8 %stats.1.lse = f32[16,8,128]{2,1,0:T(8,128)} custom-call(f32[8,128]{1,0:T(8,128)} %get-tuple-element.18.small), custom_call_target="tpu_custom_call" | custom-call | tf_op jit(solution)/shard_map/stats/pallas_call | solution.py:466
  113.1 16.4 %keys.1.gk = f32[8,64,128]{2,1,0:T(8,128)} custom-call(f32[3,8]{1,0:T(4,128)} %mix.3, bf16[128,384]{1,0:T(8,128)(2,1)} %bitcast.15, bf16[128,512]{1,0:T(8,128)(2,1)} %bitcast.11, bf16[16,128,384]{2,1,0:T(8,128)(2,1)} %get-tuple-element.16.tq_all, bf16[16,4,128,128]{3,2,1,0:T(8,128)(2,1)} %get-tuple-element.17.sq_all, f32[16,8,128]{2,1,0:T(8,128)} %stats.1.lse), custom_call_target="tpu_custom_call" | custom-call | tf_op jit(solution)/shard_map/keys/pallas_call | solution.py:472
  129.5 24.1 %sums.1 = (f32[128,64]{1,0:T(8,128)}, f32[128,64]{1,0:T(8,128)}, f32[8,128]{1,0:T(8,128)}) custom-call(f32[8,64,128]{2,1,0:T(8,128)} %get-tuple-element.15.gq, f32[8,64,128]{2,1,0:T(8,128)} %keys.1.gk, f32[16,8,128]{2,1,0:T(8,128)} %stats.1.lse), custom_call_target="tpu_custom_call" | custom-call | tf_op jit(solution)/shard_map/sums/pallas_call | solution.py:480
  153.6 1.5 copy.9
  155.2 1.5 copy.10
  156.7 1.3 multiply_bitcast_fusion
  158.0 0.7 multiply_reduce_fusion
  158.7 0.7 mul.7

commit v2 on v0

v2 whole, which is shorter than its diff:
```python
import functools
import itertools

import jax
import jax.numpy as jnp
from jax import lax
from jax.experimental import pallas as pl
from jax.experimental.pallas import tpu as pltpu
from jax.sharding import PartitionSpec as P

HEADS_T = 24
HD_T = 128
HEADS_S = 8
HD_S = 64
MESH = pl.DeviceIdType.MESH
NT = (((1,), (1,)), ((), ()))
F32 = jnp.float32
VM = pltpu.VMEM
WHOLE = pl.BlockSpec(memory_space=pltpu.VMEM)
ANY = pl.BlockSpec(memory_space=pl.ANY)
SMEM = pl.BlockSpec(memory_space=pltpu.SMEM)
COLS = 2
CHUNKS = 2
LAG = 3
GATE = 9
BEHIND = 1


def ring(axis, shift):
    n = lax.axis_size(axis)
    return lax.rem(lax.axis_index(axis) + (shift + n), n)


def remote(src, dst, send, recv, where):
    return pltpu.make_async_remote_copy(
        src_ref=src, dst_ref=dst, send_sem=send, recv_sem=recv,
        device_id=where, device_id_type=MESH)


def greet(places, while_waiting):
    barrier = pltpu.get_barrier_semaphore()
    for place in places:
        pl.semaphore_signal(barrier, inc=1, device_id=place, device_id_type=MESH)
    while_waiting()
    pl.semaphore_wait(barrier, len(places))


class Gather:
    def __init__(self, which, t_own, s_own, t_all, s_all, sems):
        self.which = which
        self.t_own, self.s_own, self.t_all, self.s_all = t_own, s_own, t_all, s_all
        self.ts, self.tr, self.zs, self.zr, self.ys, self.yr, self.local = sems
        self.n = lax.axis_size("seq")
        self.half = self.n // 2
        g = lax.axis_index("head")
        self.rows = t_own.shape[0]
        self.ny = lax.axis_size("head") // COLS
        self.y = g // COLS
        self.x = lax.rem(g, COLS)
        self.sent = []
        self.locals = [
            pltpu.make_async_copy(self.t_own, self.t_all.at[0], self.local.at[self.which, 0]),
            pltpu.make_async_copy(self.s_own, self.s_all.at[0], self.local.at[self.which, 1]),
        ]

    def y_at(self, shift):
        return lax.rem(self.y + (shift + self.ny), self.ny)

    def y_place(self, shift):
        return {"head": self.y_at(shift) * COLS + self.x}

    def slot(self, way, s):
        return 0 if s == 0 else 2 * s - 1 if way == 0 or s == self.half else 2 * s

    def t_has(self, way, s, c):
        return s < self.half or (s == self.half and way == c // (CHUNKS // 2))

    def s_has(self, way, s):
        return s < self.half or (s == self.half and way == self.which)

    def t_copy(self, way, s, c):
        step = self.rows // CHUNKS
        part = pl.ds(c * step, step)
        src = self.t_own.at[part] if s == 1 else self.t_all.at[self.slot(way, s - 1), part]
        return remote(src, self.t_all.at[self.slot(way, s), part], self.ts.at[self.which, way, s, c],
                      self.tr.at[self.which, way, s, c],
                      {"seq": ring("seq", 1 if way == 0 else -1)})

    def quarter(self, ref, q):
        return ref.at[:, pl.ds(pl.multiple_of(q * 128, 128), 128)]

    def s_copy(self, way, s):
        src = self.quarter(self.s_own, self.y) if s == 1 else self.quarter(self.s_all.at[self.slot(way, s - 1)], self.y)
        return remote(src, self.quarter(self.s_all.at[self.slot(way, s)], self.y), self.zs.at[self.which, way, s],
                      self.zr.at[self.which, way, s],
                      {"seq": ring("seq", 1 if way == 0 else -1)})

    def y_copy(self, way, s, hop):
        ref = self.quarter(self.s_all.at[self.slot(way, s)], self.y)
        return remote(ref, ref, self.ys.at[self.which, way, s, hop], self.yr.at[self.which, way, s, hop],
                      self.y_place((1, -1, 2)[hop]))

    def go(self, copy):
        copy.start()
        self.sent.append(copy)

    def ways(self, s):
        return [0] if s == 0 else [w for w in (0, 1) if self.s_has(w, s)]

    def begin(self):
        for way in (0, 1):
            if self.s_has(way, 1):
                self.go(self.s_copy(way, 1))
        for c in range(CHUNKS):
            for way in (0, 1):
                if self.t_has(way, 1, c):
                    self.go(self.t_copy(way, 1, c))

    def s_step(self, s):
        for way in self.ways(s):
            self.s_copy(way, s).wait_recv()
            if self.s_has(way, s + 1):
                self.go(self.s_copy(way, s + 1))
            for hop in range(3):
                self.go(self.y_copy(way, s, hop))

    def y_step(self, s):
        for way in self.ways(s):
            for hop in range(3):
                self.y_copy(way, s, hop).wait_recv()

    def t_step(self, s, c):
        for way in (0, 1):
            if self.t_has(way, s, c):
                self.t_copy(way, s, c).wait_recv()
                if self.t_has(way, s + 1, c):
                    self.go(self.t_copy(way, s + 1, c))

    def ticks(self, s):
        h = self.half
        if 1 <= s <= h:
            yield lambda: self.s_step(s), 0
            for c in range(CHUNKS):
                yield functools.partial(self.t_step, s, c), 0
        for a in range(1, h + 1):
            if min(a + BEHIND, h + 1) == s:
                yield functools.partial(self.y_step, a), a

    def own_here(self):
        for c in self.locals:
            c.wait()

    def finish(self):
        for c in self.sent:
            c.wait_send()


def gather_sems(n):
    half = n // 2
    dma = pltpu.SemaphoreType.DMA
    return [dma((2, 2, half + 1, CHUNKS)), dma((2, 2, half + 1, CHUNKS)), dma((2, 2, half + 1)),
            dma((2, 2, half + 1)), dma((2, 2, half + 1, 3)), dma((2, 2, half + 1, 3)), dma((2, 2))]


RB = 16
LOG = HD_T ** -0.5


def mix_row(mix, t):
    group = lax.broadcasted_iota(jnp.int32, (1, HEADS_S * HD_S), 1) // HD_S
    row = jnp.full(group.shape, mix[t, 0], F32)
    for h in range(1, HEADS_S):
        row = jnp.where(group == h, mix[t, h], row)
    return row


def weigh(mix, own, out):
    wide = own[...].astype(F32)
    rows = own.shape[0]
    for t in range(3):
        v = wide * (mix_row(mix, t) * HD_S ** -0.5)
        high = v.astype(jnp.bfloat16)
        out[0, t * rows:(t + 1) * rows, :] = high
        out[1, t * rows:(t + 1) * rows, :] = (v - high.astype(F32)).astype(jnp.bfloat16)


def logits(lo, cnt, t_own, weighed, t_all, s_all, t_map, l_map, at):
    rows = t_own.shape[0]
    lanes = slice(at * rows, (at + cnt) * rows)
    for t in range(3):
        cols = slice(t * HD_T, (t + 1) * HD_T)
        other = t_all[lo:lo + cnt, :, cols].reshape(cnt * rows, HD_T)
        t_map[t, :, lanes] = lax.dot_general(t_own[:, cols], other, NT, preferred_element_type=F32) * LOG
    other = s_all[lo:lo + cnt].reshape(cnt * rows, HEADS_S * HD_S)
    low = lax.dot_general(weighed[0], other, NT, preferred_element_type=F32)
    low = low + lax.dot_general(weighed[1], other, NT, preferred_element_type=F32)
    for t in range(3):
        l_map[t, :, lanes] = low[t * rows:(t + 1) * rows]


def online(lo, cnt, t_map, l_map, top, tot, div):
    rows = t_map.shape[1]

    def block(rb, _):
        r = pl.ds(pl.multiple_of(rb * RB, RB), RB)
        for t in range(3):
            a = [t_map[t, r, (lo + i) * rows:(lo + i + 1) * rows] for i in range(cnt)]
            b = [l_map[t, r, (lo + i) * rows:(lo + i + 1) * rows] for i in range(cnt)]
            new = functools.reduce(jnp.maximum, a, top[t, r, :])
            fade = jnp.exp(top[t, r, :] - new)
            ea = [jnp.exp(v - new) for v in a]
            top[t, r, :] = new
            tot[t, r, :] = tot[t, r, :] * fade + sum(ea[1:], ea[0])
            terms = [e * (u - v) for e, u, v in zip(ea, a, b)]
            div[t, r, :] = div[t, r, :] * fade + sum(terms[1:], terms[0])
            new = functools.reduce(jnp.maximum, b, top[3 + t, r, :])
            fade = jnp.exp(top[3 + t, r, :] - new)
            eb = [jnp.exp(v - new) for v in b]
            top[3 + t, r, :] = new
            tot[3 + t, r, :] = tot[3 + t, r, :] * fade + sum(eb[1:], eb[0])
        return 0

    lax.fori_loop(0, rows // RB, block, 0)


def settle(top, tot, div, stat):
    shape = stat.shape
    lane = lax.broadcasted_iota(jnp.int32, shape, 1)
    tile = jnp.zeros(shape, F32)
    lse, fade, tots = [], [], []
    for k in range(6):
        m = top[k]
        best = jnp.max(m, axis=-1, keepdims=True)
        f = jnp.exp(m - best)
        s = jnp.sum(tot[k] * f, axis=-1, keepdims=True)
        lse.append(best + jnp.log(s))
        fade.append(f)
        tots.append(s)
    for k in range(6):
        wide = jnp.broadcast_to(lse[k], shape)
        top[k] = wide
        tile = jnp.where(lane == k, wide, tile)
    for t in range(3):
        d = jnp.sum(div[t] * fade[t], axis=-1, keepdims=True) / tots[t] - lse[t] + lse[3 + t]
        tile = jnp.where(lane == 8 + t, d, tile)
    stat[...] = tile
    return stat[...].T


def fold(weights, ex):
    return [weights[0][h] * ex[0] + weights[1][h] * ex[1] + weights[2][h] * ex[2] for h in range(HEADS_S)]


def excess(lo, cnt, mix, t_map, l_map, lse_of, ex, back):
    rows = t_map.shape[1]
    weights = [[mix[t, h] for h in range(HEADS_S)] for t in range(3)]

    def block(rb, _):
        r = pl.ds(pl.multiple_of(rb * RB, RB), RB)
        for i in range(cnt):
            lanes = slice((lo + i) * rows, (lo + i + 1) * rows)
            here = slice(i * rows, (i + 1) * rows)
            v = [jnp.exp(l_map[t, r, lanes] - lse_of(3 + t, i, r)) - jnp.exp(t_map[t, r, lanes] - lse_of(t, i, r))
                 for t in range(3)]
            for h, b in enumerate(fold(weights, v)):
                back[h, r, here] = b.astype(jnp.bfloat16)
            if ex is not None:
                for t in range(3):
                    ex[pl.ds(pl.multiple_of(t * rows + rb * RB, RB), RB), here] = v[t].astype(jnp.bfloat16)
        return 0

    lax.fori_loop(0, rows // RB, block, 0)


def heads_up(lo, cnt, back, s_all, acc, first):
    rows = s_all.shape[1]
    for h in range(HEADS_S):
        other = s_all[lo:lo + cnt, :, h * HD_S:(h + 1) * HD_S].reshape(cnt * rows, HD_S)
        v = jnp.dot(back[h, :, 0:cnt * rows], other, preferred_element_type=F32)
        acc[h] = v if first else acc[h] + v


def gather_up(lo, cnt, ex, s_all, acc, first):
    rows = s_all.shape[1]
    v = jnp.dot(ex[:, 0:cnt * rows], s_all[lo:lo + cnt].reshape(cnt * rows, HEADS_S * HD_S), preferred_element_type=F32)
    acc[...] = v if first else acc[...] + v


def combine(acc, factor, out):
    for h in range(HEADS_S):
        out[h] = (acc[h] * factor).T


def mix_sums(acc, sq, turned, out):
    rows = sq.shape[0]
    wide = sq[...].astype(F32)
    sub = lax.broadcasted_iota(jnp.int32, (8, 128), 0)
    lane = lax.broadcasted_iota(jnp.int32, (8, 128), 1)
    lines = [jnp.sum(acc[t * rows:(t + 1) * rows, :] * wide, axis=0, keepdims=True) for t in range(3)]
    tile = jnp.zeros((8, 128), F32)
    for t in range(3):
        own = jnp.sum(turned[8 + t:9 + t, :], axis=-1, keepdims=True)
        tile = jnp.where((sub == 3) & (lane == t), own, tile)
    for q in range(4):
        v = jnp.zeros((8, 128), F32)
        for t in range(3):
            v = jnp.where(sub == t, lines[t][:, q * 128:(q + 1) * 128], v)
        for k in range(2):
            own = jnp.sum(jnp.where(lane // HD_S == k, v, 0.0), axis=-1, keepdims=True) * HD_S ** -0.5
            tile = jnp.where((lane == 2 * q + k) & (sub < 3), own, tile)
    out[...] = tile


class Plan:
    def __init__(self, blocks, key_block, lse_in):
        self.soon, self.later = [], []
        self.blocks, self.key_block, self.lse_in = blocks, key_block, lse_in
        self.units, self.done, self.since = 0, 0, None

    def sent(self, lse_out):
        lse_out()
        self.since = 0

    def have(self, all_of_it):
        self.units = 2 * self.blocks if all_of_it else self.units + 1

    def key_side(self):
        if self.done == self.blocks or self.units < min(2 * self.done + 2, 2 * self.blocks):
            return False
        if self.lse_in:
            self.lse_in()
            self.lse_in = None
        self.key_block(4 * self.done, 4)
        self.done += 1
        return True

    def step(self):
        if self.since is not None:
            self.since += 1
        if self.soon:
            self.soon.pop(0)()
        elif self.later:
            self.later.pop(0)()
        elif self.since is not None and self.since >= GATE:
            self.key_side()

    def drain(self):
        while self.soon or self.later:
            (self.soon or self.later).pop(0)()
        while self.key_side():
            pass


def main_kernel(factor, mix, tk, sk, tq, sq, got, tiles,
                tk_all, sk_all, tq_all, sq_all, mq, mk, t_map, l_map, t_map2, l_map2, top, tot, div, ex, back, x_acc, q_acc, k_acc, stat,
                own_lse, lse_all, own_sum, sums_all, dp_sum, gq, gk, *sems):
    n = lax.axis_size("seq")
    heads, dps = lax.axis_size("head"), lax.axis_size("dp")
    z, g, d = lax.axis_index("seq"), lax.axis_index("head"), lax.axis_index("dp")
    half = n // 2
    lsend, lrecv, msend, mrecv, dsend, drecv, rsend, rrecv, own_sems = sems[7:]
    key = Gather(0, tk, sk, tk_all, sk_all, sems[:7])
    query = Gather(1, tq, sq, tq_all, sq_all, sems[:7])
    held = {}
    sent = []

    def unit(s):
        return (0, 1) if s == 0 else (2 * s - 1, 1 if s == half else 2)

    def row_unit(s):
        lo, cnt = unit(s)
        logits(lo, cnt, tq, mq, tk_all, sk_all, t_map, l_map, lo)
        online(lo, cnt, t_map, l_map, top, tot, div)

    def row_block(b):
        excess(4 * b, 4, mix, t_map, l_map, lambda k, i, r: top[k, r, :], ex, back)
        heads_up(4 * b, 4, back, sk_all, q_acc, b == 0)
        gather_up(4 * b, 4, ex, sk_all, x_acc, b == 0)

    def key_logits(s):
        lo, cnt = unit(s)
        logits(lo, cnt, tk, mk, tq_all, sq_all, t_map2, l_map2, lo)

    def key_block(lo, cnt):
        wide = [[jnp.broadcast_to(lse_all[lo + i, k:k + 1, :], (RB, 128)) for k in range(6)] for i in range(cnt)]
        excess(lo, cnt, mix, t_map2, l_map2, lambda k, i, r: wide[i][k], None, back)
        heads_up(lo, cnt, back, sq_all, k_acc, lo == 0)

    def first():
        for c in key.locals + query.locals:
            c.start()
        weigh(mix, sq, mq)
        weigh(mix, sk, mk)
        top[...] = jnp.full_like(top, -1e30)
        tot[...] = jnp.zeros_like(tot)
        div[...] = jnp.zeros_like(div)
        key.own_here()
        query.own_here()
        row_unit(0)

    def spread(copies):
        for c in copies:
            c.start()
            sent.append(c)

    def lse_copy(o):
        place = 2 * o - 1 if o <= half else 2 * (n - o)
        return remote(own_lse, lse_all.at[place], lsend.at[o], lrecv.at[o], {"seq": ring("seq", o)})

    def sum_copy(o, at):
        return remote(own_sum, sums_all.at[at], msend.at[o], mrecv.at[o], {"seq": ring("seq", o)})

    def dp_copy(o, at):
        return remote(dp_sum, tiles.at[at], dsend.at[o], drecv.at[o], {"dp": ring("dp", o)})

    def slice_copy(k, ref, o):
        to = ring("head", o)
        return remote(ref.at[to], got.at[k, o], rsend.at[k, o], rrecv.at[k, o], {"head": to})

    def keep(copy):
        copy.start()
        return copy

    def lse_ready():
        held["turned"] = settle(top, tot, div, stat)
        own_lse[...] = held["turned"][0:8, :]

    def lse_out():
        held["lse"] = keep(pltpu.make_async_copy(own_lse, lse_all.at[0], own_sems.at[0]))
        spread(lse_copy(o) for o in range(1, n))

    def row_end():
        mix_sums(x_acc, sq, held["turned"], own_sum)
        combine(q_acc, factor, gq)

    def row_out():
        held["sum"] = keep(pltpu.make_async_copy(own_sum, sums_all.at[z], own_sems.at[1]))
        held["gq"] = keep(pltpu.make_async_copy(gq.at[g], got.at[1, 0], own_sems.at[2]))
        spread(sum_copy(o, z) for o in range(1, n))
        spread(slice_copy(1, gq, o) for o in range(1, heads))

    def lse_in():
        held["lse"].wait()
        for o in range(1, n):
            lse_copy(o).wait_recv()

    def total_of_images():
        held["sum"].wait()
        for o in range(1, n):
            sum_copy(o, z).wait_recv()
        total = sums_all[0]
        for j in range(1, n):
            total = total + sums_all[j]
        dp_sum[...] = total

    def dp_out():
        held["dp"] = keep(pltpu.make_async_copy(dp_sum, tiles.at[d], own_sems.at[1]))
        spread(dp_copy(o, d) for o in range(1, dps))

    greet([{"seq": ring("seq", o)} for o in (1, n - 1)] + [{"head": ring("head", o)} for o in range(1, heads)]
          + [{"dp": ring("dp", o)} for o in range(1, dps)], first)
    key.begin()
    plan = Plan(n // 4, key_block, lse_in)
    plan.later.append(functools.partial(key_logits, 0))
    def arrived(k, q):
        if k:
            plan.soon.append(functools.partial(row_unit, k))
            if k == half:
                plan.soon += [lse_ready, lambda: plan.sent(lse_out)]
                plan.soon += [functools.partial(row_block, b) for b in range(n // 4)]
                plan.soon += [row_end, lambda: None, row_out]
        if q:
            plan.later.append(functools.partial(key_logits, q))
            plan.later.append(functools.partial(plan.have, q == half))

    for i in range(1, half + 3 + LAG):
        if i == LAG:
            query.begin()
        for k, q in itertools.zip_longest(key.ticks(i), query.ticks(i - LAG)):
            if k:
                k[0]()
                arrived(k[1], 0)
                plan.step()
            if q:
                q[0]()
                arrived(0, q[1])
                plan.step()
    plan.drain()
    total_of_images()
    combine(k_acc, factor, gk)
    dp_out()
    key.finish()
    query.finish()
    held["gk"] = keep(pltpu.make_async_copy(gk.at[g], got.at[0, 0], own_sems.at[0]))
    spread(slice_copy(0, gk, o) for o in range(1, heads))
    for name in ("gq", "dp", "gk"):
        held[name].wait()
    for o in range(1, heads):
        slice_copy(1, gq, o).wait_recv()
    for o in range(1, dps):
        dp_copy(o, d).wait_recv()
    for o in range(1, heads):
        slice_copy(0, gk, o).wait_recv()
    for c in sent:
        c.wait_send()


def last_kernel(scale_mix, scale_loss, got, tiles, out_q, out_k, out_mix, out_loss):
    for k, out in enumerate((out_k, out_q)):
        acc = got[k, 0]
        for o in range(1, got.shape[1]):
            acc = acc + got[k, o]
        out[...] = acc
    total = tiles[0]
    for j in range(1, tiles.shape[0]):
        total = total + tiles[j]
    out_mix[...] = total[0:3, 0:8] * scale_mix
    out_loss[...] = total[3, 0:3] * scale_loss


def body(teacher_query, teacher_key, student_query, student_key, head_mix):
    n = lax.axis_size("seq")
    tq, sq, tk, sk = teacher_query[0], student_query[0], teacher_key[0], student_key[0]
    rows = tq.shape[0]
    bf = jnp.bfloat16
    dma = pltpu.SemaphoreType.DMA
    seq_len = rows * n
    weight = seq_len / HEADS_T
    factor = weight * HD_S ** -0.5
    images = lax.axis_size("dp")
    heads = lax.axis_size("head")
    width = HEADS_S * HD_S
    t_all, s_all = VM((n, *tq.shape), bf), VM((n, *sq.shape), bf)
    weighed = VM((2, 3 * rows, width), bf)
    got, tiles = pl.pallas_call(
        functools.partial(main_kernel, factor),
        out_shape=(jax.ShapeDtypeStruct((2, heads, HD_S, rows), F32), jax.ShapeDtypeStruct((images, 8, 128), F32)),
        in_specs=[SMEM] + [WHOLE] * 4, out_specs=[ANY] * 2, name="main",
        scratch_shapes=[
            t_all, s_all, t_all, s_all, weighed, weighed,
            *[VM((3, rows, n * rows), F32)] * 4,
            VM((6, rows, 128), F32), VM((6, rows, 128), F32), VM((3, rows, 128), F32),
            VM((3 * rows, 4 * rows), bf), VM((HEADS_S, rows, 4 * rows), bf), VM((3 * rows, width), F32),
            VM((HEADS_S, rows, HD_S), F32), VM((HEADS_S, rows, HD_S), F32),
            VM((rows, 128), F32), VM((8, 128), F32), VM((n, 8, 128), F32),
            VM((8, 128), F32), VM((n, 8, 128), F32), VM((8, 128), F32),
            VM((HEADS_S, HD_S, rows), F32), VM((HEADS_S, HD_S, rows), F32),
        ] + gather_sems(n) + [dma((n,)), dma((n,)), dma((n,)), dma((n,)), dma((images,)), dma((images,)),
                              dma((2, heads)), dma((2, heads)), dma((3,))],
        compiler_params=pltpu.CompilerParams(collective_id=0, has_side_effects=True),
    )(head_mix, tk, sk, tq, sq)
    out = jax.ShapeDtypeStruct((HD_S, rows), F32)
    out_q, out_k, out_mix, out_loss = pl.pallas_call(
        functools.partial(last_kernel, weight / (images * seq_len), 1.0 / (images * seq_len)),
        out_shape=(out, out, jax.ShapeDtypeStruct((3, 8), F32), jax.ShapeDtypeStruct((3,), F32)),
        in_specs=[WHOLE] * 2, out_specs=[WHOLE] * 4, name="last",
    )(got, tiles)
    return out_q.T[None], out_k.T[None], out_mix, out_loss


def solution(mesh):
    return jax.shard_map(
        body,
        mesh=mesh,
        in_specs=(
            P("dp", "seq", "head"),
            P("dp", "seq", "head"),
            P("dp", "seq", None),
            P("dp", "seq", None),
            P("head", None),
        ),
        out_specs=(P("dp", "seq", "head"), P("dp", "seq", "head"), P("head", None), P("head")),
        check_vma=False,
    )
```

time: 526 us -> 88.7 us (0.17)
  the two profiles are of different devices: /device:TPU:1 before, /device:TPU:4 now
where the time goes in v2:
time: 88.7 us; the launch traced here: 88.5 us
  Pallas kernels  87.9 us (99%)
    pallas_call x1, Pallas kernels, body(): pl.pallas_call(functools.partial(main_kernel, factor), out_shape=(jax.Sha...  86.2 us

profile of v2, /device:TPU:4, one launch (start us, length us, event | category | flops | bytes accessed | tf_op | source)
XLA Modules:
  0.0 88.5 jit_solution(1484986465904149111)
XLA Ops:
  0.6 86.2 %main.1 = (f32[2,8,64,128]{3,2,1,0:T(8,128)}, f32[4,8,128]{2,1,0:T(8,128)}) custom-call(f32[3,8]{1,0:T(4,128)} %mix.1, bf16[128,384]{1,0:T(8,128)(2,1)} %bitcast.12, bf16[128,512]{1,0:T(8,128)(2,1)} %bitcast.10, bf16[128,384]{1,0:T(8,128)(2,1)} %bitcast.13, bf16[128,512]{1,0:T(8,128)(2,1)} %bitcast.11), custom_call_target="tpu_custom_call" | custom-call | tf_op jit(solution)/shard_map/main/pallas_call | solution.py:535
  86.8 1.7 %last.1 = (f32[64,128]{1,0:T(8,128)}, f32[64,128]{1,0:T(8,128)}, f32[3,8]{1,0:T(4,128)}, f32[3]{0:T(128)}) custom-call(f32[2,8,64,128]{3,2,1,0:T(8,128)} %get-tuple-element.10.got, f32[4,8,128]{2,1,0:T(8,128)} %get-tuple-element.11.tiles), custom_call_target="tpu_custom_call" | custom-call | tf_op jit(solution)/shard_map/last/pallas_call | solution.py:553
